TPU v7x, 32 devices: a whole 2x2x4 slice. The times are simulated.
32 devices in a mesh: group: 2 (over y), dp: 8 (over z, x), tensor: 2 (over core).
Axes of the slice: x: 2, y: 2, z: 4, core: 2. Of those that a mesh axis runs over, the one named last changes fastest.
Arguments:
- inputs: bfloat16 [12288, 1536], P(('group', 'dp')), may hold values from -6 to 6
- cotangent: bfloat16 [12288, 1536], P(('group', 'dp')), may hold values from -6 to 6
- lengths: int32 [16, 3], P(('group', 'dp')), may hold values from 1 to 576, 768 in all within a row
- attn_gain: bfloat16 [1536], P('dp'), may hold values from 0.25 to 1.75
- w_query: bfloat16 [1536, 1536], P('dp', 'tensor'), may hold values from -0.15625 to 0.15625
- b_query: bfloat16 [1536], P('tensor'), may hold values from -3 to 3
- w_key: bfloat16 [1536, 256], P('dp', 'tensor'), may hold values from -0.15625 to 0.15625
- b_key: bfloat16 [256], P('tensor'), may hold values from -3 to 3
- w_value: bfloat16 [1536, 256], P('dp', 'tensor'), may hold values from -0.15625 to 0.15625
- b_value: bfloat16 [256], P('tensor'), may hold values from -3 to 3
- w_out: bfloat16 [1536, 1536], P('dp', 'tensor'), may hold values from -1.25 to 1.25
- ffn_gain: bfloat16 [1536], P('dp'), may hold values from 0.25 to 1.75
- w_gate: bfloat16 [1536, 8960], P('dp', 'tensor'), may hold values from -0.15625 to 0.15625
- w_up: bfloat16 [1536, 8960], P('dp', 'tensor'), may hold values from -0.15625 to 0.15625
- w_down: bfloat16 [1536, 8960], P('dp', 'tensor'), may hold values from -0.0625 to 0.0625
Outputs:
- layer_out: bfloat16 [12288, 1536], P(('group', 'dp'))
- input_grad: bfloat16 [12288, 1536], P(('group', 'dp'))
- attn_gain_grad: float32 [1536], P('dp')
- w_query_grad: float32 [1536, 1536], P('dp', 'tensor')
- b_query_grad: float32 [1536], P('tensor')
- w_key_grad: float32 [1536, 256], P('dp', 'tensor')
- b_key_grad: float32 [256], P('tensor')
- w_value_grad: float32 [1536, 256], P('dp', 'tensor')
- b_value_grad: float32 [256], P('tensor')
- w_out_grad: float32 [1536, 1536], P('dp', 'tensor')
- ffn_gain_grad: float32 [1536], P('dp')
- w_gate_grad: float32 [1536, 8960], P('dp', 'tensor')
- w_up_grad: float32 [1536, 8960], P('dp', 'tensor')
- w_down_grad: float32 [1536, 8960], P('dp', 'tensor')
Inputs may be any that keep to these rules, and one draw needn't show every extreme that they name: In every stream the 3 lengths sum to 768, and the longest is exactly 576.
All inputs are finite; a program needn't handle non-finite values.
Results may differ from a plain program's by a relative error of at most 0.017.
Values may be sent and summed in bfloat16 or wider, within the bound.
No kernel may reach another device: no remote copies, remote signals or barrier semaphores. Data moves between devices by JAX's collectives and lax.ppermute only.
A program may use at most 384 MiB of HBM per device.

v0:
```python
import math
import jax
import jax.numpy as jnp
from jax import lax
from jax.sharding import PartitionSpec as P

HD = 128
SEQ = 768
NSEG = 3
EPSILON = 1e-06
THETA = 10000.0
MASKED_SCORE = -1e30


def normalize(values):
    return values * lax.rsqrt(jnp.mean(values * values, axis=-1, keepdims=True) + EPSILON)


def scaled_norm(values, gain_vec):
    return normalize(values) * gain_vec


def rotate(values, cosine, sine_table):
    half_width = values.shape[-1] // 2
    turned = jnp.concatenate([-values[..., half_width:], values[..., :half_width]], axis=-1)
    return values * cosine + turned * sine_table


def unrotate(values, cosine, sine_table):
    half_width = values.shape[-1] // 2
    sined = values * sine_table
    turned = jnp.concatenate([sined[..., half_width:], -sined[..., :half_width]], axis=-1)
    return values * cosine + turned


def layout(lengths):
    segment_ends = jnp.cumsum(lengths, axis=-1)
    segment_starts = segment_ends - lengths
    places = jnp.arange(SEQ, dtype=jnp.int32)
    segment = jnp.sum((places[:, None] >= segment_ends[..., None, :]).astype(jnp.int32), axis=-1)
    choose = segment[..., None] == jnp.arange(NSEG, dtype=jnp.int32)
    picked = jnp.sum(jnp.where(choose, segment_starts[..., None, :], 0), axis=-1)
    return (segment, places - picked)


def angles(position):
    frequency = jnp.exp(-(math.log(THETA) * 2.0 / HD) * jnp.arange(HD // 2, dtype=jnp.float32))
    phase_angle = position.astype(jnp.float32)[..., None] * frequency
    phase_angle = jnp.concatenate([phase_angle, phase_angle], axis=-1)
    return (jnp.cos(phase_angle), jnp.sin(phase_angle))


def plain_dot(left_side, right_side):
    return jnp.dot(left_side, right_side, preferred_element_type=jnp.float32)


def trans_dot(left_side, right_side):
    return lax.dot_general(
        left_side, right_side, (((1,), (1,)), ((), ())), preferred_element_type=jnp.float32
    )


def outer_dot(left_side, right_side):
    return lax.dot_general(
        left_side, right_side, (((0,), (0,)), ((), ())), preferred_element_type=jnp.float32
    )


def masked_scores(queries, keys_rot, allowed):
    raw_scores = jnp.einsum("qkgd,skd->kgqs", queries, keys_rot, preferred_element_type=jnp.float32)
    return jnp.where(allowed, raw_scores * HD ** (-0.5), MASKED_SCORE)


AXES = ("group", "dp", "tensor")


def routes(dp_count):

    def table(move):
        flat = lambda g, d, t: (g * dp_count + d) * 2 + t
        return [
            (flat(g, d, t), flat(*move(g, d, t)))
            for g in range(2)
            for d in range(dp_count)
            for t in range(2)
        ]

    return {
        "x": table(lambda g, d, t: (g, d ^ 1, t)),
        "y": table(lambda g, d, t: (g ^ 1, d, t)),
        "t": table(lambda g, d, t: (g, d, t ^ 1)),
        "first": table(lambda g, d, t: (g, d ^ 1, t) if t == 0 else (g ^ 1, d, t)),
        "second": table(lambda g, d, t: (g ^ 1, d, t) if t == 0 else (g, d ^ 1, t)),
    }


def local(
    inputs,
    cotangent,
    lengths,
    attn_gain,
    w_query,
    b_query,
    w_key,
    b_key,
    w_value,
    b_value,
    w_out,
    ffn_gain,
    w_gate,
    w_up,
    w_down,
):
    bf16 = jnp.bfloat16
    f32 = jnp.float32
    dp_count = lax.axis_size("dp")
    line = dp_count // 2
    dp_index = lax.axis_index("dp")
    x_index = dp_index % 2
    y_index = lax.axis_index("group")
    core = lax.axis_index("tensor")
    table = routes(dp_count)
    line_groups = [[2 * z + x for z in range(line)] for x in range(2)]
    tokens, d_model = inputs.shape
    half = tokens // 2
    rows = w_query.shape[0]
    head_count = w_query.shape[1] // HD
    kv_count = w_key.shape[1] // HD
    group_size = head_count // kv_count
    ffn_cols = w_gate.shape[1]
    quarter = -(-ffn_cols // 512) * 128
    score_scale = HD ** (-0.5)

    def send(value, route):
        return lax.ppermute(value, AXES, table[route])

    def pick(value, index):
        return lax.dynamic_index_in_dim(value, index, 0, keepdims=False)

    def in_order(index, mine, other):
        first = index == 0
        return (jnp.where(first, mine, other), jnp.where(first, other, mine))

    def my_half(value):
        return pick(value.reshape(2, half, value.shape[-1]), core)

    def other_half(value):
        return pick(value.reshape(2, half, value.shape[-1]), 1 - core)

    def both_halves(mine):
        return jnp.concatenate(in_order(core, mine, send(mine, "t")), axis=0)

    def square_gather(mine):
        near = send(mine, "first")
        mine_sib = send(mine, "t")
        far = send(jnp.stack([mine, near]), "second")
        near_sib = send(near, "t")
        far_sib = send(far, "t")
        return jnp.concatenate(
            [mine, near, far[0], far[1], mine_sib, near_sib, far_sib[0], far_sib[1]], axis=0
        )

    def square_scatter(mine, theirs):
        came = send(theirs.astype(bf16), "t")
        total = (mine.astype(f32) + came.astype(f32)).reshape(4, half, d_model)
        came = send(total[2:].astype(bf16), "second")
        total = total[:2] + came.astype(f32)
        came = send(total[1].astype(bf16), "first")
        return total[0] + came.astype(f32)

    def ffn_gather(weight):
        padded = jnp.pad(weight, ((0, 0), (0, 4 * quarter - ffn_cols)))
        parts = padded.reshape(rows, 4, quarter).transpose(1, 0, 2)
        mine = pick(parts, x_index * 2 + y_index)
        came = send(pick(parts, (1 - x_index) * 2 + y_index), "x")
        pair = jnp.stack(in_order(x_index, mine, came))
        full = lax.all_gather(pair, "dp", axis=0, axis_index_groups=line_groups)
        return full.reshape(d_model, quarter)

    def ffn_scatter(grad):
        parts = grad.astype(bf16).reshape(line, 2 * rows, quarter)
        summed = lax.psum_scatter(
            parts, "dp", scatter_dimension=0, axis_index_groups=line_groups
        ).reshape(2, rows, quarter)
        came = send(pick(summed, 1 - x_index), "x")
        pair = jnp.stack(in_order(x_index, pick(summed, x_index), came))
        low, high = in_order(y_index, pair, send(pair, "y"))
        whole = jnp.concatenate([low[0], high[0], low[1], high[1]], axis=1)
        return whole[:, :ffn_cols].astype(f32)

    def attn_scatter(grad):
        summed = lax.psum_scatter(grad.astype(bf16), "dp", scatter_dimension=0, tiled=True)
        return summed.astype(f32) + send(summed, "y").astype(f32)

    stream = inputs.astype(f32)
    segment, position = layout(lengths[0])
    cosine, sine_table = angles(position)
    cosine = cosine[:, None, :]
    sine_table = sine_table[:, None, :]
    places = jnp.arange(SEQ, dtype=jnp.int32)
    allowed = (segment[:, None] == segment[None, :]) & (places[None, :] <= places[:, None])
    gains = jnp.pad(jnp.stack([attn_gain, ffn_gain], axis=1), ((0, 0), (0, 126)))
    query_cols = head_count * HD
    key_cols = kv_count * HD
    qkv_cols = query_cols + 2 * key_cols
    qkv_full = lax.all_gather(
        jnp.concatenate([w_query, w_key, w_value, gains], axis=1), "dp", axis=0, tiled=True
    )
    out_full = lax.all_gather(w_out, "dp", axis=0, tiled=True)
    gate_full = ffn_gather(w_gate)
    up_full = ffn_gather(w_up)
    down_full = ffn_gather(w_down)
    cot_half = my_half(cotangent)
    cot_all = square_gather(cot_half)
    gain_one = qkv_full[:, qkv_cols].astype(f32)
    gain_two = qkv_full[:, qkv_cols + 1].astype(f32)
    qkv_full = qkv_full[:, :qkv_cols]
    inv_one = lax.rsqrt(jnp.mean(stream * stream, axis=-1, keepdims=True) + EPSILON)
    h_one = (stream * inv_one * gain_one).astype(bf16)
    qkv_bias = jnp.concatenate([b_query, b_key, b_value]).astype(f32)
    qkv_pre = plain_dot(h_one, qkv_full) + qkv_bias
    query_pre = qkv_pre[:, :query_cols]
    key_pre = qkv_pre[:, query_cols : query_cols + key_cols]
    value_pre = qkv_pre[:, query_cols + key_cols :]
    queries = rotate(query_pre.reshape(SEQ, head_count, HD), cosine, sine_table).astype(bf16)
    queries = queries.reshape(SEQ, kv_count, group_size, HD)
    keys_rot = rotate(key_pre.reshape(SEQ, kv_count, HD), cosine, sine_table).astype(bf16)
    values_low = value_pre.astype(bf16).reshape(SEQ, kv_count, HD)
    scores = masked_scores(queries, keys_rot, allowed)
    row_max = jnp.max(scores, axis=-1, keepdims=True)
    exp_terms = jnp.exp(scores - row_max)
    row_total = jnp.sum(exp_terms, axis=-1, keepdims=True)
    log_total = row_max + jnp.log(row_total)
    probs_low = (exp_terms / row_total).astype(bf16)
    attended = jnp.einsum("kgqs,skd->qkgd", probs_low, values_low, preferred_element_type=f32)
    attended = attended.reshape(SEQ, head_count * HD).astype(bf16)
    branch = trans_dot(attended, out_full)
    resid = (
        my_half(stream) + my_half(branch) + send(other_half(branch).astype(bf16), "t").astype(f32)
    )
    inv_two = lax.rsqrt(jnp.mean(resid * resid, axis=-1, keepdims=True) + EPSILON)
    norm_two = resid * inv_two
    h_two = square_gather((norm_two * gain_two).astype(bf16))
    gate_pre = plain_dot(h_two, gate_full)
    up_pre = plain_dot(h_two, up_full)
    sigmoid_gate = jax.nn.sigmoid(gate_pre)
    swish_gate = gate_pre * sigmoid_gate
    hidden = (swish_gate * up_pre).astype(bf16)
    down_grad = ffn_scatter(outer_dot(cot_all, hidden))
    d_hidden = plain_dot(cot_all, down_full)
    d_gate = (d_hidden * up_pre * sigmoid_gate * (1.0 + gate_pre * (1.0 - sigmoid_gate))).astype(
        bf16
    )
    d_up = (d_hidden * swish_gate).astype(bf16)
    mid = 4 * half

    def entry(part):
        return trans_dot(d_gate[part], gate_full) + trans_dot(d_up[part], up_full)

    d_h_two = square_scatter(entry(slice(0, mid)), entry(slice(mid, None)))
    gate_grad = ffn_scatter(outer_dot(h_two, d_gate))
    up_grad = ffn_scatter(outer_dot(h_two, d_up))
    ffn_total = square_scatter(
        trans_dot(hidden[:mid], down_full), trans_dot(hidden[mid:], down_full)
    )
    layer_out = both_halves((resid + ffn_total).astype(bf16))
    scaled = d_h_two * gain_two
    d_resid = cot_half.astype(f32) + inv_two * (
        scaled - norm_two * jnp.mean(norm_two * scaled, axis=-1, keepdims=True)
    )
    gain_two_part = jnp.sum(d_h_two * norm_two, axis=0)
    d_out_low = both_halves(d_resid.astype(bf16))
    out_grad = attn_scatter(outer_dot(d_out_low, attended))
    d_attended = plain_dot(d_out_low, out_full).astype(bf16).reshape(SEQ, kv_count, group_size, HD)
    scores = masked_scores(queries, keys_rot, allowed)
    probabilities = jnp.exp(scores - log_total)
    d_probs = jnp.einsum("qkgd,skd->kgqs", d_attended, values_low, preferred_element_type=f32)
    d_value = jnp.einsum(
        "kgqs,qkgd->skd", probabilities.astype(bf16), d_attended, preferred_element_type=f32
    )
    d_value = d_value.reshape(SEQ, kv_count * HD).astype(bf16)
    d_scores = probabilities * (d_probs - jnp.sum(probabilities * d_probs, axis=-1, keepdims=True))
    d_scores = d_scores.astype(bf16)
    d_query_rot = (
        jnp.einsum("kgqs,skd->qkgd", d_scores, keys_rot, preferred_element_type=f32) * score_scale
    )
    d_key_rot = (
        jnp.einsum("kgqs,qkgd->skd", d_scores, queries, preferred_element_type=f32) * score_scale
    )
    d_query = (
        unrotate(d_query_rot.reshape(SEQ, head_count, HD), cosine, sine_table)
        .astype(bf16)
        .reshape(SEQ, head_count * HD)
    )
    d_key = unrotate(d_key_rot, cosine, sine_table).astype(bf16).reshape(SEQ, kv_count * HD)
    d_qkv = jnp.concatenate([d_query, d_key, d_value], axis=1)
    qkv_grad = attn_scatter(outer_dot(h_one, d_qkv))
    entry_one = trans_dot(d_qkv, qkv_full)
    d_h_one = my_half(entry_one) + send(other_half(entry_one).astype(bf16), "t").astype(f32)
    half_inv = my_half(inv_one)
    norm_one = my_half(stream) * half_inv
    scaled = d_h_one * gain_one
    input_grad = both_halves(
        (
            d_resid
            + half_inv * (scaled - norm_one * jnp.mean(norm_one * scaled, axis=-1, keepdims=True))
        ).astype(bf16)
    )
    gain_one_part = jnp.sum(d_h_one * norm_one, axis=0)
    bias_part = jnp.sum(d_qkv.astype(f32), axis=0)
    small = jnp.concatenate([gain_one_part, gain_two_part, bias_part]).reshape(-1, 128)
    small = small + send(small, "y")
    step = 1
    while step < dp_count:
        small = small + lax.ppermute(small, "dp", [(i, i ^ step) for i in range(dp_count)])
        step *= 2
    small = small.reshape(-1)
    gain_sums = small[: 2 * d_model].reshape(2, dp_count, rows)
    mine = lax.dynamic_index_in_dim(gain_sums, dp_index, 1, keepdims=False)
    mine = mine + send(mine, "t")
    bias_sum = small[2 * d_model :]
    return (
        layer_out,
        input_grad,
        mine[0],
        qkv_grad[:, :query_cols],
        bias_sum[:query_cols],
        qkv_grad[:, query_cols : query_cols + key_cols],
        bias_sum[query_cols : query_cols + key_cols],
        qkv_grad[:, query_cols + key_cols :],
        bias_sum[query_cols + key_cols :],
        out_grad,
        mine[1],
        gate_grad,
        up_grad,
        down_grad,
    )


def solution(mesh):
    in_specs = (
        P(("group", "dp"), None),
        P(("group", "dp"), None),
        P(("group", "dp"), None),
        P("dp"),
        P("dp", "tensor"),
        P("tensor"),
        P("dp", "tensor"),
        P("tensor"),
        P("dp", "tensor"),
        P("tensor"),
        P("dp", "tensor"),
        P("dp"),
        P("dp", "tensor"),
        P("dp", "tensor"),
        P("dp", "tensor"),
    )
    out_specs = (
        P(("group", "dp"), None),
        P(("group", "dp"), None),
        P("dp"),
        P("dp", "tensor"),
        P("tensor"),
        P("dp", "tensor"),
        P("tensor"),
        P("dp", "tensor"),
        P("tensor"),
        P("dp", "tensor"),
        P("dp"),
        P("dp", "tensor"),
        P("dp", "tensor"),
        P("dp", "tensor"),
    )
    return jax.shard_map(local, mesh=mesh, in_specs=in_specs, out_specs=out_specs, check_vma=False)
```

profile of v0, /device:TPU:0, one launch (start us, length us, event | category | flops | bytes accessed | tf_op | source)
XLA Modules:
  0.0 870.4 jit_solution(2815979763971457537)
XLA Ops:
  17.0 6.6 constant_dynamic-slice_fusion.4
  26.7 11.8 %collective-permute-done.7 = bf16[192,1152]{1,0:T(8,128)(2,1)S(1)} collective-permute-done((bf16[192,1152]{1,0:T(8,128)(2,1)S(1)}, bf16[192,1152]{1,0:T(8,128)(2,1)S(1)}, u32[]{:S(2)}, u32[]{:S(2)}) %collective-permute-start.7) | collective-permute-done | bytes 442400 | tf_op jit(solution)/shard_map/ppermute | solution.py:135
  52.6 14.3 %collective-permute-done.6 = bf16[192,1152]{1,0:T(8,128)(2,1)} collective-permute-done((bf16[192,1152]{1,0:T(8,128)(2,1)}, bf16[192,1152]{1,0:T(8,128)(2,1)}, u32[]{:S(2)}, u32[]{:S(2)}) %collective-permute-start.6) | collective-permute-done | bytes 442400 | tf_op jit(solution)/shard_map/ppermute | solution.py:135
  69.3 22.2 %all-gather.9.cloned.1.call-done = bf16[1536,1152]{1,0:T(8,128)(2,1)} async-done(((bf16[192,1152]{1,0:T(8,128)(2,1)}), bf16[1536,1152]{1,0:T(8,128)(2,1)}) %all-gather.9.cloned.1.call-update) | async-done | bytes 3538960 | tf_op jit(solution)/shard_map/all_gather | solution.py:206
  133.5 10.9 %all-gather.11.cloned.1.call-done = bf16[1536,768]{1,0:T(8,128)(2,1)} async-done(((bf16[192,768]{1,0:T(8,128)(2,1)}), bf16[1536,768]{1,0:T(8,128)(2,1)}) %all-gather.11.cloned.1.call-update) | async-done | bytes 2359312 | tf_op jit(solution)/shard_map/all_gather | solution.py:209
  158.3 6.8 collective-permute-done.8
  165.2 26.8 %collective-permute-done.14 = bf16[2,384,1536]{2,1,0:T(8,128)(2,1)} collective-permute-done((bf16[2,384,1536]{2,1,0:T(8,128)(2,1)S(1)}, bf16[2,384,1536]{2,1,0:T(8,128)(2,1)}, u32[]{:S(2)}, u32[]{:S(2)}) %collective-permute-start.14) | collective-permute-done | bytes 2359328 | tf_op jit(solution)/shard_map/ppermute | solution.py:135
  192.0 9.2 %collective-permute-start.17 = (bf16[2,384,1536]{2,1,0:T(8,128)(2,1)}, bf16[2,384,1536]{2,1,0:T(8,128)(2,1)}, u32[]{:S(2)}, u32[]{:S(2)}) collective-permute-start(bf16[2,384,1536]{2,1,0:T(8,128)(2,1)} %collective-permute-done.14), channel_id=1, source_target_pairs={{0,1},{1,0},{2,3},{3,2},{4,5},{5,4},{6,7},{7,6},{8,9},{9,8},{10,11... | collective-permute-start | bytes 7077896 | tf_op jit(solution)/shard_map/ppermute | solution.py:135
  215.9 15.6 %collective-permute-done.2 = bf16[2,384,1536]{2,1,0:T(8,128)(2,1)S(1)} collective-permute-done((bf16[2,384,1536]{2,1,0:T(8,128)(2,1)S(1)}, bf16[2,384,1536]{2,1,0:T(8,128)(2,1)S(1)}, u32[]{:S(2)}, u32[]{:S(2)}) %collective-permute-start.2) | collective-permute-done | bytes 2359328 | tf_op jit(solution)/shard_map/ppermute | solution.py:135
  242.7 17.9 %fusion.106 = f32[3072,1152]{1,0:T(8,128)} fusion(bf16[3072,1536]{1,0:T(8,128)(2,1)} %fusion.60, bf16[1536,1152]{1,0:T(8,128)(2,1)} %bitcast.411), kind=kOutput, calls=%fused_computation.271 | convolution fusion | flops 10871635968 | bytes 27131904 | tf_op jit(solution)/shard_map/dot_general | solution.py:54
  260.6 24.4 %all-gather.13.cloned.1.call-done = bf16[8,192,1152]{2,1,0:T(8,128)(2,1)} async-done(((bf16[2,192,1152]{2,1,0:T(8,128)(2,1)}), bf16[8,192,1152]{2,1,0:T(8,128)(2,1)}) %all-gather.13.cloned.1.call-update) | async-done | bytes 3538960 | tf_op jit(solution)/shard_map/all_gather | solution.py:177
  285.0 17.9 %fusion.105 = f32[3072,1152]{1,0:T(8,128)} fusion(bf16[3072,1536]{1,0:T(8,128)(2,1)} %fusion.60, bf16[1536,1152]{1,0:T(8,128)(2,1)} %bitcast.414), kind=kOutput, calls=%fused_computation.270 | convolution fusion | flops 10871635968 | bytes 27131904 | tf_op jit(solution)/shard_map/dot_general | solution.py:54
  302.9 52.7 %all-gather.17.cloned.1.call-done = bf16[8,192,1152]{2,1,0:T(8,128)(2,1)} async-done(((bf16[2,192,1152]{2,1,0:T(8,128)(2,1)}), bf16[8,192,1152]{2,1,0:T(8,128)(2,1)}) %all-gather.17.cloned.1.call-update) | async-done | bytes 3538960 | tf_op jit(solution)/shard_map/all_gather | solution.py:177
  355.6 29.6 %multiply_convert_fusion = (bf16[3072,1152]{1,0:T(8,128)(2,1)}, bf16[3072,1152]{1,0:T(8,128)(2,1)}, bf16[3072,1152]{1,0:T(8,128)(2,1)}) fusion(f32[3072,1152]{1,0:T(8,128)} %fusion.105, f32[3072,1152]{1,0:T(8,128)} %fusion.106, bf16[3072,1536]{1,0:T(8,128)(2,1)} %fusion.56, bf16[1536,1152]{1,0:T(8,128)(2,1)} %bitcast.417), kind=kOutput, calls=%fused_computation.7 | convolution fusion | flops 10924720128 | bytes 62521344 | tf_op jit(solution)/shard_map/dot_general | solution.py:54
  385.2 18.1 %convolution_convert_fusion.1 = bf16[1536,1152]{1,0:T(8,128)(2,1)} fusion(bf16[3072,1536]{1,0:T(8,128)(2,1)} %fusion.56, bf16[3072,1152]{1,0:T(8,128)(2,1)} %get-tuple-element.30), kind=kOutput, calls=%fused_computation.20 | convolution fusion | flops 10873405440 | bytes 20054016 | tf_op jit(solution)/shard_map/dot_general | solution.py:64
  403.3 18.0 %convolution_convert_fusion.2 = bf16[1536,1152]{1,0:T(8,128)(2,1)} fusion(bf16[3072,1536]{1,0:T(8,128)(2,1)} %fusion.60, bf16[3072,1152]{1,0:T(8,128)(2,1)} %get-tuple-element.28), kind=kOutput, calls=%fused_computation.21 | convolution fusion | flops 10873405440 | bytes 20054016 | tf_op jit(solution)/shard_map/dot_general | solution.py:64
  421.4 10.9 %convolution_convert_fusion = bf16[1536,1536]{1,0:T(8,128)(2,1)} fusion(bf16[1536,1152]{1,0:T(8,128)(2,1)} %bitcast.418, bf16[3072,1152]{1,0:T(8,128)(2,1)} %get-tuple-element.30), kind=kOutput, calls=%fused_computation.19 | convolution fusion | flops 5438177280 | bytes 11796480 | tf_op jit(solution)/shard_map/dot_general | solution.py:58
  432.3 11.0 %fusion.14 = f32[1536,1536]{1,0:T(8,128)} fusion(bf16[1536,1152]{1,0:T(8,128)(2,1)S(1)} %bitcast.416, bf16[3072,1152]{1,0:T(8,128)(2,1)} %get-tuple-element.29), kind=kOutput, calls=%fused_computation.37 | convolution fusion | flops 5435817984 | bytes 16515072 | tf_op jit(solution)/shard_map/dot_general | solution.py:58
  443.3 11.6 %add_convert_fusion = bf16[1536,1536]{1,0:T(8,128)(2,1)} fusion(f32[1536,1536]{1,0:T(8,128)} %fusion.14, bf16[1536,1152]{1,0:T(8,128)(2,1)S(1)} %bitcast.413, bf16[3072,1152]{1,0:T(8,128)(2,1)} %get-tuple-element.28), kind=kOutput, calls=%fused_computation.17 | convolution fusion | flops 5440536576 | bytes 21233664 | tf_op jit(solution)/shard_map/dot_general | solution.py:58
  455.4 14.6 %convolution_convert_fusion.3 = bf16[1536,1152]{1,0:T(8,128)(2,1)} fusion(bf16[3072,1536]{1,0:T(8,128)(2,1)S(1)} %bitcast.406, bf16[3072,1152]{1,0:T(8,128)(2,1)S(1)} %bitcast.422), kind=kOutput, calls=%fused_computation.22 | convolution fusion | flops 10873405440 | bytes 20054016 | tf_op jit(solution)/shard_map/dot_general | solution.py:64
  470.7 12.0 %fusion.17 = f32[1536,1536]{1,0:T(8,128)} fusion(bf16[1536,1152]{1,0:T(8,128)(2,1)} %bitcast.415, bf16[3072,1152]{1,0:T(8,128)(2,1)} %get-tuple-element.29), kind=kOutput, calls=%fused_computation.40 | convolution fusion | flops 5435817984 | bytes 16515072 | tf_op jit(solution)/shard_map/dot_general | solution.py:58
  482.7 8.7 %convert_add_fusion.1 = f32[1536,1536]{1,0:T(8,128)S(1)} fusion(bf16[1536,1536]{1,0:T(8,128)(2,1)} %collective-permute-done.9, bf16[1536,1152]{1,0:T(8,128)(2,1)S(1)} %bitcast.419, bf16[3072,1152]{1,0:T(8,128)(2,1)} %get-tuple-element.30), kind=kOutput, calls=%fused_computation.18 | convolution fusion | flops 5440536576 | bytes 21233664 | tf_op jit(solution)/shard_map/dot_general | solution.py:58
  494.6 12.3 %convert_add_fusion = f32[1536,1536]{1,0:T(8,128)S(1)} fusion(bf16[1536,1536]{1,0:T(8,128)(2,1)} %collective-permute-done.18, f32[1536,1536]{1,0:T(8,128)} %fusion.17, bf16[1536,1152]{1,0:T(8,128)(2,1)} %bitcast.412, bf16[3072,1152]{1,0:T(8,128)(2,1)} %get-tuple-element.28), kind=kOutput, calls=%fused_computation.16 | convolution fusion | flops 5442895872 | bytes 30670848 | tf_op jit(solution)/shard_map/dot_general | solution.py:58
  515.3 22.2 %reduce-scatter.12.cloned.1.call-done = bf16[1,384,1152]{2,1,0:T(8,128)(2,1)} async-done(((bf16[4,384,1152]{2,1,0:T(8,128)(2,1)}), bf16[1,384,1152]{2,1,0:T(8,128)(2,1)}) %reduce-scatter.12.cloned.1.call-update) | async-done | bytes 884752 | tf_op jit(solution)/shard_map/reduce_scatter | solution.py:182
  540.1 66.4 %reduce-scatter.10.cloned.1.call-done = bf16[1,384,1152]{2,1,0:T(8,128)(2,1)} async-done(((bf16[4,384,1152]{2,1,0:T(8,128)(2,1)}), bf16[1,384,1152]{2,1,0:T(8,128)(2,1)}) %reduce-scatter.10.cloned.1.call-update) | async-done | bytes 884752 | tf_op jit(solution)/shard_map/reduce_scatter | solution.py:182
  622.5 22.0 %collective-permute-done.20 = bf16[384,1536]{1,0:T(8,128)(2,1)S(1)} collective-permute-done((bf16[384,1536]{1,0:T(8,128)(2,1)S(1)}, bf16[384,1536]{1,0:T(8,128)(2,1)S(1)}, u32[]{:S(2)}, u32[]{:S(2)}) %collective-permute-start.20) | collective-permute-done | bytes 1179680 | tf_op jit(solution)/shard_map/ppermute | solution.py:135
  648.6 14.7 %collective-permute-start.21 = (bf16[384,1536]{1,0:T(8,128)(2,1)S(1)}, bf16[384,1536]{1,0:T(8,128)(2,1)S(1)}, u32[]{:S(2)}, u32[]{:S(2)}) collective-permute-start(bf16[384,1536]{1,0:T(8,128)(2,1)S(1)} %get-tuple-element.20), channel_id=1, source_target_pairs={{0,1},{1,0},{2,3},{3,2},{4,5},{5,4},{6,7},{7,6},{8,9},{9,8},{10,11... | collective-permute-start | bytes 3538952 | tf_op jit(solution)/shard_map/ppermute | solution.py:135
  670.1 8.8 %collective-permute-done.32 = bf16[2,192,1152]{2,1,0:T(8,128)(2,1)S(1)} collective-permute-done((bf16[2,192,1152]{2,1,0:T(8,128)(2,1)S(1)}, bf16[2,192,1152]{2,1,0:T(8,128)(2,1)S(1)}, u32[]{:S(2)}, u32[]{:S(2)}) %collective-permute-start.32) | collective-permute-done | bytes 884768 | tf_op jit(solution)/shard_map/ppermute | solution.py:135
  690.9 12.0 %fusion = (f32[6,768]{1,0:T(8,128)S(1)}, f32[768,768,6]{1,0,2:T(8,128)}) fusion(f32[1,6,768,768]{2,3,1,0:T(8,128)} %copy-done, f32[6,768]{1,0:T(8,128)S(1)} %log_add_fusion, bf16[768,6,128]{0,2,1:T(8,128)(2,1)S(1)} %bitcast.387, f32[768,1024]{1,0:T(8,128)} %copy-done.10), kind=kOutput, calls=%fused_computation.3 | convolution fusion | flops 916581888 | bytes 29724672 | tf_op jit(solution)/shard_map/qkgd,skd->kgqs/dot_general | solution.py:277
  705.4 7.8 fusion.9
  741.9 18.4 %collective-permute-start.22 = (bf16[384,1536]{1,0:T(8,128)(2,1)S(1)}, bf16[384,1536]{1,0:T(8,128)(2,1)S(1)}, u32[]{:S(2)}, u32[]{:S(2)}) collective-permute-start(bf16[384,1536]{1,0:T(8,128)(2,1)S(1)} %fusion.53), channel_id=1, source_target_pairs={{0,1},{1,0},{2,3},{3,2},{4,5},{5,4},{6,7},{7,6},{8,9},{9,8},{10,11... | collective-permute-start | bytes 3538952 | tf_op jit(solution)/shard_map/ppermute | solution.py:135
  784.6 66.6 %reduce-scatter.6.cloned.1.call-done = bf16[192,1024]{1,0:T(8,128)(2,1)} async-done(((bf16[1536,1024]{1,0:T(8,128)(2,1)}), bf16[192,1024]{1,0:T(8,128)(2,1)}) %reduce-scatter.6.cloned.1.call-update) | async-done | bytes 393232 | tf_op jit(solution)/shard_map/reduce_scatter | solution.py:192
  (389 shorter events, 231.8 us)
Async XLA Ops:
  7.2 84.4 %all-gather.9.cloned.1.call-start = ((), (), s32[]{:S(2)}) async-start(), calls=%async_computation.5 | async-start | bytes 3981312 | tf_op jit(solution)/shard_map/all_gather | solution.py:206
  10.6 133.9 %all-gather.11.cloned.1.call-start = ((), (), s32[]{:S(2)}) async-start(), calls=%async_computation.6 | async-start | bytes 2654208 | tf_op jit(solution)/shard_map/all_gather | solution.py:209
  11.3 231.4 %all-gather.15.cloned.1.call-start = ((), (), s32[]{:S(2)}) async-start(), calls=%async_computation.13 | async-start | bytes 4423680 | tf_op jit(solution)/shard_map/all_gather | solution.py:177
  39.6 245.4 %all-gather.13.cloned.1.call-start = ((), (), s32[]{:S(2)}) async-start(), calls=%async_computation.12 | async-start | bytes 4423680 | tf_op jit(solution)/shard_map/all_gather | solution.py:177
  44.5 22.4 %collective-permute-start.6 = (bf16[192,1152]{1,0:T(8,128)(2,1)}, bf16[192,1152]{1,0:T(8,128)(2,1)}, u32[]{:S(2)}, u32[]{:S(2)}) collective-permute-start(bf16[192,1152]{1,0:T(8,128)(2,1)} %bitcast.368), channel_id=1, source_target_pairs={{0,2},{1,3},{2,0},{3,1},{4,6},{5,7},{6,4},{7,5},{8,10},{9,11},{10,... | collective-permute-start | bytes 1327112 | tf_op jit(solution)/shard_map/ppermute | solution.py:135
  47.7 100.7 %collective-permute-start.13 = (bf16[384,1536]{1,0:T(8,128)(2,1)}, bf16[384,1536]{1,0:T(8,128)(2,1)}, u32[]{:S(2)}, u32[]{:S(2)}) collective-permute-start(bf16[384,1536]{1,0:T(8,128)(2,1)} %bitcast.49), channel_id=1, source_target_pairs={{0,2},{1,17},{2,0},{3,19},{4,6},{5,21},{6,4},{7,23},{8,10},{9,25},... | collective-permute-start | bytes 3538952 | tf_op jit(solution)/shard_map/ppermute | solution.py:135
  69.1 286.5 %all-gather.17.cloned.1.call-start = ((), (), s32[]{:S(2)}) async-start(), calls=%async_computation.14 | async-start | bytes 4423680 | tf_op jit(solution)/shard_map/all_gather | solution.py:177
  150.4 41.7 %collective-permute-start.14 = (bf16[2,384,1536]{2,1,0:T(8,128)(2,1)S(1)}, bf16[2,384,1536]{2,1,0:T(8,128)(2,1)}, u32[]{:S(2)}, u32[]{:S(2)}) collective-permute-start(bf16[2,384,1536]{2,1,0:T(8,128)(2,1)S(1)} %pad_maximum_fusion.2), channel_id=1, source_target_pairs={{0,16},{1,3},{2,18},{3,1},{4,20},{5,7},{6,22},{7,5},{8,24},{9,11},... | collective-permute-start | bytes 7077896 | tf_op jit(solution)/shard_map/ppermute | solution.py:135
  156.8 45.6 %collective-permute-start.1 = (bf16[384,1536]{1,0:T(8,128)(2,1)S(1)}, bf16[384,1536]{1,0:T(8,128)(2,1)S(1)}, u32[]{:S(2)}, u32[]{:S(2)}) collective-permute-start(bf16[384,1536]{1,0:T(8,128)(2,1)S(1)} %get-tuple-element.25), channel_id=1, source_target_pairs={{0,2},{1,17},{2,0},{3,19},{4,6},{5,21},{6,4},{7,23},{8,10},{9,25},... | collective-permute-start | bytes 3538952 | tf_op jit(solution)/shard_map/ppermute | solution.py:135
  158.3 53.0 %collective-permute-start.15 = (bf16[384,1536]{1,0:T(8,128)(2,1)}, bf16[384,1536]{1,0:T(8,128)(2,1)S(1)}, u32[]{:S(2)}, u32[]{:S(2)}) collective-permute-start(bf16[384,1536]{1,0:T(8,128)(2,1)} %bitcast.49), channel_id=1, source_target_pairs={{0,1},{1,0},{2,3},{3,2},{4,5},{5,4},{6,7},{7,6},{8,9},{9,8},{10,11... | collective-permute-start | bytes 3538952 | tf_op jit(solution)/shard_map/ppermute | solution.py:135
  192.0 21.5 %collective-permute-start.17 = (bf16[2,384,1536]{2,1,0:T(8,128)(2,1)}, bf16[2,384,1536]{2,1,0:T(8,128)(2,1)}, u32[]{:S(2)}, u32[]{:S(2)}) collective-permute-start(bf16[2,384,1536]{2,1,0:T(8,128)(2,1)} %collective-permute-done.14), channel_id=1, source_target_pairs={{0,1},{1,0},{2,3},{3,2},{4,5},{5,4},{6,7},{7,6},{8,9},{9,8},{10,11... | collective-permute-start | bytes 7077896 | tf_op jit(solution)/shard_map/ppermute | solution.py:135
  202.3 310.5 %reduce-scatter.14.cloned.1.call-start = ((), (), s32[]{:S(2)}) async-start(), calls=%async_computation.11 | async-start | bytes 4423680 | tf_op jit(solution)/shard_map/reduce_scatter | solution.py:182
  202.6 28.9 %collective-permute-start.2 = (bf16[2,384,1536]{2,1,0:T(8,128)(2,1)S(1)}, bf16[2,384,1536]{2,1,0:T(8,128)(2,1)S(1)}, u32[]{:S(2)}, u32[]{:S(2)}) collective-permute-start(bf16[2,384,1536]{2,1,0:T(8,128)(2,1)S(1)} %pad_maximum_fusion), channel_id=1, source_target_pairs={{0,16},{1,3},{2,18},{3,1},{4,20},{5,7},{6,22},{7,5},{8,24},{9,11},... | collective-permute-start | bytes 7077896 | tf_op jit(solution)/shard_map/ppermute | solution.py:135
  403.3 134.3 %reduce-scatter.12.cloned.1.call-start = ((), (), s32[]{:S(2)}) async-start(), calls=%async_computation.10 | async-start | bytes 4423680 | tf_op jit(solution)/shard_map/reduce_scatter | solution.py:182
  421.4 185.2 %reduce-scatter.10.cloned.1.call-start = ((), (), s32[]{:S(2)}) async-start(), calls=%async_computation.9 | async-start | bytes 4423680 | tf_op jit(solution)/shard_map/reduce_scatter | solution.py:182
  432.3 50.5 %collective-permute-start.9 = (bf16[1536,1536]{1,0:T(8,128)(2,1)}, bf16[1536,1536]{1,0:T(8,128)(2,1)}, u32[]{:S(2)}, u32[]{:S(2)}) collective-permute-start(bf16[1536,1536]{1,0:T(8,128)(2,1)} %convolution_convert_fusion), channel_id=1, source_target_pairs={{0,1},{1,0},{2,3},{3,2},{4,5},{5,4},{6,7},{7,6},{8,9},{9,8},{10,11... | collective-permute-start | bytes 14155784 | tf_op jit(solution)/shard_map/ppermute | solution.py:135
  454.9 39.7 %collective-permute-start.18 = (bf16[1536,1536]{1,0:T(8,128)(2,1)}, bf16[1536,1536]{1,0:T(8,128)(2,1)}, u32[]{:S(2)}, u32[]{:S(2)}) collective-permute-start(bf16[1536,1536]{1,0:T(8,128)(2,1)} %add_convert_fusion), channel_id=1, source_target_pairs={{0,1},{1,0},{2,3},{3,2},{4,5},{5,4},{6,7},{7,6},{8,9},{9,8},{10,11... | collective-permute-start | bytes 14155784 | tf_op jit(solution)/shard_map/ppermute | solution.py:135
  470.0 313.0 %reduce-scatter.8.cloned.1.call-start = ((), (), s32[]{:S(2)}) async-start(), calls=%async_computation.8 | async-start | bytes 2654208 | tf_op jit(solution)/shard_map/reduce_scatter | solution.py:192
  493.2 116.0 %collective-permute-start.10 = (bf16[2,384,1536]{2,1,0:T(8,128)(2,1)}, bf16[2,384,1536]{2,1,0:T(8,128)(2,1)}, u32[]{:S(2)}, u32[]{:S(2)}) collective-permute-start(bf16[2,384,1536]{2,1,0:T(8,128)(2,1)} %bitcast.45), channel_id=1, source_target_pairs={{0,16},{1,3},{2,18},{3,1},{4,20},{5,7},{6,22},{7,5},{8,24},{9,11},... | collective-permute-start | bytes 7077896 | tf_op jit(solution)/shard_map/ppermute | solution.py:135
  508.9 105.0 %collective-permute-start.19 = (bf16[2,384,1536]{2,1,0:T(8,128)(2,1)}, bf16[2,384,1536]{2,1,0:T(8,128)(2,1)}, u32[]{:S(2)}, u32[]{:S(2)}) collective-permute-start(bf16[2,384,1536]{2,1,0:T(8,128)(2,1)} %bitcast.56), channel_id=1, source_target_pairs={{0,16},{1,3},{2,18},{3,1},{4,20},{5,7},{6,22},{7,5},{8,24},{9,11},... | collective-permute-start | bytes 7077896 | tf_op jit(solution)/shard_map/ppermute | solution.py:135
  513.8 104.4 %collective-permute-start.35 = (bf16[192,1152]{1,0:T(8,128)(2,1)S(1)}, bf16[192,1152]{1,0:T(8,128)(2,1)S(1)}, u32[]{:S(2)}, u32[]{:S(2)}) collective-permute-start(bf16[192,1152]{1,0:T(8,128)(2,1)S(1)} %dynamic-slice_bitcast_fusion), channel_id=1, source_target_pairs={{0,2},{1,3},{2,0},{3,1},{4,6},{5,7},{6,4},{7,5},{8,10},{9,11},{10,... | collective-permute-start | bytes 1327112 | tf_op jit(solution)/shard_map/ppermute | solution.py:135
  538.6 81.3 %collective-permute-start.33 = (bf16[192,1152]{1,0:T(8,128)(2,1)S(1)}, bf16[192,1152]{1,0:T(8,128)(2,1)S(1)}, u32[]{:S(2)}, u32[]{:S(2)}) collective-permute-start(bf16[192,1152]{1,0:T(8,128)(2,1)S(1)} %dynamic-slice_bitcast_fusion.1), channel_id=1, source_target_pairs={{0,2},{1,3},{2,0},{3,1},{4,6},{5,7},{6,4},{7,5},{8,10},{9,11},{10,... | collective-permute-start | bytes 1327112 | tf_op jit(solution)/shard_map/ppermute | solution.py:135
  613.4 31.9 %collective-permute-start.11 = (bf16[384,1536]{1,0:T(8,128)(2,1)S(1)}, bf16[384,1536]{1,0:T(8,128)(2,1)S(1)}, u32[]{:S(2)}, u32[]{:S(2)}) collective-permute-start(bf16[384,1536]{1,0:T(8,128)(2,1)S(1)} %fusion.54), channel_id=1, source_target_pairs={{0,2},{1,17},{2,0},{3,19},{4,6},{5,21},{6,4},{7,23},{8,10},{9,25},... | collective-permute-start | bytes 3538952 | tf_op jit(solution)/shard_map/ppermute | solution.py:135
  616.6 27.9 %collective-permute-start.20 = (bf16[384,1536]{1,0:T(8,128)(2,1)S(1)}, bf16[384,1536]{1,0:T(8,128)(2,1)S(1)}, u32[]{:S(2)}, u32[]{:S(2)}) collective-permute-start(bf16[384,1536]{1,0:T(8,128)(2,1)S(1)} %fusion.55), channel_id=1, source_target_pairs={{0,2},{1,17},{2,0},{3,19},{4,6},{5,21},{6,4},{7,23},{8,10},{9,25},... | collective-permute-start | bytes 3538952 | tf_op jit(solution)/shard_map/ppermute | solution.py:135
  618.4 44.9 %collective-permute-start.36 = (bf16[2,192,1152]{2,1,0:T(8,128)(2,1)S(1)}, bf16[2,192,1152]{2,1,0:T(8,128)(2,1)}, u32[]{:S(2)}, u32[]{:S(2)}) collective-permute-start(bf16[2,192,1152]{2,1,0:T(8,128)(2,1)S(1)} %pad_maximum_fusion.23), channel_id=1, source_target_pairs={{0,16},{1,17},{2,18},{3,19},{4,20},{5,21},{6,22},{7,23},{8,24},{9,... | collective-permute-start | bytes 2654216 | tf_op jit(solution)/shard_map/ppermute | solution.py:135
  620.1 44.6 %collective-permute-start.34 = (bf16[2,192,1152]{2,1,0:T(8,128)(2,1)S(1)}, bf16[2,192,1152]{2,1,0:T(8,128)(2,1)}, u32[]{:S(2)}, u32[]{:S(2)}) collective-permute-start(bf16[2,192,1152]{2,1,0:T(8,128)(2,1)S(1)} %pad_maximum_fusion.22), channel_id=1, source_target_pairs={{0,16},{1,17},{2,18},{3,19},{4,20},{5,21},{6,22},{7,23},{8,24},{9,... | collective-permute-start | bytes 2654216 | tf_op jit(solution)/shard_map/ppermute | solution.py:135
  620.9 58.0 %collective-permute-start.32 = (bf16[2,192,1152]{2,1,0:T(8,128)(2,1)S(1)}, bf16[2,192,1152]{2,1,0:T(8,128)(2,1)S(1)}, u32[]{:S(2)}, u32[]{:S(2)}) collective-permute-start(bf16[2,192,1152]{2,1,0:T(8,128)(2,1)S(1)} %pad_maximum_fusion.21), channel_id=1, source_target_pairs={{0,16},{1,17},{2,18},{3,19},{4,20},{5,21},{6,22},{7,23},{8,24},{9,... | collective-permute-start | bytes 2654216 | tf_op jit(solution)/shard_map/ppermute | solution.py:135
  648.6 32.6 %collective-permute-start.21 = (bf16[384,1536]{1,0:T(8,128)(2,1)S(1)}, bf16[384,1536]{1,0:T(8,128)(2,1)S(1)}, u32[]{:S(2)}, u32[]{:S(2)}) collective-permute-start(bf16[384,1536]{1,0:T(8,128)(2,1)S(1)} %get-tuple-element.20), channel_id=1, source_target_pairs={{0,1},{1,0},{2,3},{3,2},{4,5},{5,4},{6,7},{7,6},{8,9},{9,8},{10,11... | collective-permute-start | bytes 3538952 | tf_op jit(solution)/shard_map/ppermute | solution.py:135
  663.2 102.0 %collective-permute-start.12 = (bf16[384,1536]{1,0:T(8,128)(2,1)}, bf16[384,1536]{1,0:T(8,128)(2,1)}, u32[]{:S(2)}, u32[]{:S(2)}) collective-permute-start(bf16[384,1536]{1,0:T(8,128)(2,1)} %get-tuple-element.37), channel_id=1, source_target_pairs={{0,1},{1,0},{2,3},{3,2},{4,5},{5,4},{6,7},{7,6},{8,9},{9,8},{10,11... | collective-permute-start | bytes 3538952 | tf_op jit(solution)/shard_map/ppermute | solution.py:135
  686.4 164.7 %reduce-scatter.6.cloned.1.call-start = ((), (), s32[]{:S(2)}) async-start(), calls=%async_computation.7 | async-start | bytes 3538944 | tf_op jit(solution)/shard_map/reduce_scatter | solution.py:192
  741.9 20.9 %collective-permute-start.22 = (bf16[384,1536]{1,0:T(8,128)(2,1)S(1)}, bf16[384,1536]{1,0:T(8,128)(2,1)S(1)}, u32[]{:S(2)}, u32[]{:S(2)}) collective-permute-start(bf16[384,1536]{1,0:T(8,128)(2,1)S(1)} %fusion.53), channel_id=1, source_target_pairs={{0,1},{1,0},{2,3},{3,2},{4,5},{5,4},{6,7},{7,6},{8,9},{9,8},{10,11... | collective-permute-start | bytes 3538952 | tf_op jit(solution)/shard_map/ppermute | solution.py:135
  783.0 71.1 %collective-permute-start.30 = (bf16[192,768]{1,0:T(8,128)(2,1)}, bf16[192,768]{1,0:T(8,128)(2,1)S(1)}, u32[]{:S(2)}, u32[]{:S(2)}) collective-permute-start(bf16[192,768]{1,0:T(8,128)(2,1)} %reduce-scatter.8.cloned.1.call-done), channel_id=1, source_target_pairs={{0,16},{1,17},{2,18},{3,19},{4,20},{5,21},{6,22},{7,23},{8,24},{9,... | collective-permute-start | bytes 884744 | tf_op jit(solution)/shard_map/ppermute | solution.py:135
  (89 other events, 904.6 us)
Sparse Core Ops, SparseCore 0:
  10.7 80.7 all-gather.8
  93.7 50.6 all-gather.10
  146.0 68.4 all-gather.14
  216.5 68.5 all-gather.12
  287.0 68.5 all-gather.16
  403.4 65.0 reduce-scatter.13
  470.8 66.6 reduce-scatter.11
  539.8 66.6 reduce-scatter.9
  686.5 87.1 reduce-scatter.7
  777.1 73.9 reduce-scatter.5
where the time goes:
time: 877 us; the launch traced here: 870 us
  waiting for transfers between devices  384 us (44%)
  matrix products  240 us (27%)
  local copies, waits for them, and re-layouts  87.7 us (10%)
  starting transfers between devices  76.5 us (9%)
  other arithmetic  66.3 us (8%)
  between operations  15.9 us (2%)
    ppermute x34, waiting for transfers between devices, send(): return lax.ppermute(value, AXES, table[route])  114 us
    reduce_scatter x3, waiting for transfers between devices, ffn_scatter(): lax.psum_scatter(parts, 'dp', scatter_dimension=0, axis_index_groups=line...  88.7 us
    all_gather x3, waiting for transfers between devices, ffn_gather(): full = lax.all_gather(pair, 'dp', axis=0, axis_index_groups=line_groups)  77.1 us
    dot_general x8, matrix products, trans_dot(): lax.dot_general(left_side, right_side, (((1,), (1,)), ((), ())), preferre...  75.4 us
    dot_general x5, matrix products, plain_dot(): return jnp.dot(left_side, right_side, preferred_element_type=jnp.float32)  74.3 us
    ppermute x34, starting transfers between devices, send(): return lax.ppermute(value, AXES, table[route])  70.9 us
    reduce_scatter x2, waiting for transfers between devices, attn_scatter(): lax.psum_scatter(grad.astype(bf16), 'dp', scatter_dimension=0, tiled=True)  66.6 us
    dot_general x5, matrix products, outer_dot(): lax.dot_general(left_side, right_side, (((0,), (0,)), ((), ())), preferre...  59.6 us
  transfers between devices with their start and end apart: 47, of which 21 were waited for; matrix products, arithmetic and copies ran while one was open for 38% of the time, Pallas kernels for 0%

commit v1 on v0

--- a/solution.py
+++ b/solution.py
@@ -203,9 +203,25 @@
     query_cols = head_count * HD
     key_cols = kv_count * HD
     qkv_cols = query_cols + 2 * key_cols
-    qkv_full = lax.all_gather(
-        jnp.concatenate([w_query, w_key, w_value, gains], axis=1), "dp", axis=0, tiled=True
-    )
+    array = jnp.concatenate([w_query, w_key, w_value, gains], axis=1)
+    count, index_2, rows_2 = (lax.axis_size("dp"), lax.axis_index("dp"), array.shape[0])
+    right = [(i_2, (i_2 + 1) % count) for i_2 in range(count)]
+    left = [(i_2, (i_2 - 1) % count) for i_2 in range(count)]
+    out = jnp.zeros((*array.shape[:0], count * rows_2, *array.shape[0 + 1 :]), array.dtype)
+    out = lax.dynamic_update_slice_in_dim(out, array, index_2 * rows_2, axis=0)
+    from_left = from_right = array
+    middle = count // 2
+    for step_2 in range(1, middle + 1):
+        from_left = lax.ppermute(from_left, "dp", right)
+        out = lax.dynamic_update_slice_in_dim(
+            out, from_left, (index_2 - step_2) % count * rows_2, axis=0
+        )
+        if step_2 < count - middle:
+            from_right = lax.ppermute(from_right, "dp", left)
+            out = lax.dynamic_update_slice_in_dim(
+                out, from_right, (index_2 + step_2) % count * rows_2, axis=0
+            )
+    qkv_full = out
     out_full = lax.all_gather(w_out, "dp", axis=0, tiled=True)
     gate_full = ffn_gather(w_gate)
     up_full = ffn_gather(w_up)

time: 877 us -> 922 us (1.051)
  local copies, waits for them, and re-layouts: 87.7 us -> 153 us
  waiting for transfers between devices: 384 us -> 343 us
  starting transfers between devices: 76.5 us -> 94.4 us
    all_gather x3, waiting for transfers between devices: 77.1 us -> 6.92 us  [ffn_gather(): full = lax.all_gather(pair, 'dp', axis=0, axis_index_groups=line_groups)]
    ppermute x0 -> x7, waiting for transfers between devices: none -> 68.3 us  [the longest x4 68.3 us: local(): from_left = lax.ppermute(from_left, 'dp', right)]
    dynamic_update_slice x0 -> x8, local copies, waits for them, and re-layouts: none -> 56.3 us  [the longest x4 27.7 us: local(): lax.dynamic_update_slice_in_dim(out, from_left, (index_2 - step_2) % coun...]
    all_gather x1 -> x0, waiting for transfers between devices: 22.2 us -> none  [local(): lax.all_gather(jnp.concatenate([w_query, w_key, w_value, gains], axis=1),...]
    ppermute x0 -> x7, starting transfers between devices: none -> 18.3 us  [the longest x3 13.4 us: local(): from_right = lax.ppermute(from_right, 'dp', left)]
    ppermute x34, waiting for transfers between devices: 114 us -> 100 us  [send(): return lax.ppermute(value, AXES, table[route])]
    all_gather x1, waiting for transfers between devices: 10.9 us -> 0.02 us  [local(): out_full = lax.all_gather(w_out, 'dp', axis=0, tiled=True)]
    unnamed x164 -> x180, local copies, waits for them, and re-layouts: 37.1 us -> 36.6 us
  transfers between devices with their start and end apart: 47 -> 53, of which waited for: 21 -> 19; matrix products, arithmetic and copies ran while one was open for 38% -> 43% of each run, Pallas kernels for 0% -> 0%
where the time goes in v1:
time: 922 us; the launch traced here: 912 us
  waiting for transfers between devices  343 us (37%)
  matrix products  242 us (26%)
  local copies, waits for them, and re-layouts  153 us (17%)
  starting transfers between devices  94.4 us (10%)
  other arithmetic  64.3 us (7%)
  between operations  15.5 us (2%)
    ppermute x34, waiting for transfers between devices, send(): return lax.ppermute(value, AXES, table[route])  100 us
    reduce_scatter x3, waiting for transfers between devices, ffn_scatter(): lax.psum_scatter(parts, 'dp', scatter_dimension=0, axis_index_groups=line...  95.8 us
    dot_general x8, matrix products, trans_dot(): lax.dot_general(left_side, right_side, (((1,), (1,)), ((), ())), preferre...  75.9 us
    dot_general x5, matrix products, plain_dot(): return jnp.dot(left_side, right_side, preferred_element_type=jnp.float32)  74.6 us
    ppermute x34, starting transfers between devices, send(): return lax.ppermute(value, AXES, table[route])  70.2 us
    ppermute x4, waiting for transfers between devices, local(): from_left = lax.ppermute(from_left, 'dp', right)  68.3 us
    reduce_scatter x2, waiting for transfers between devices, attn_scatter(): lax.psum_scatter(grad.astype(bf16), 'dp', scatter_dimension=0, tiled=True)  67.1 us
    dot_general x5, matrix products, outer_dot(): lax.dot_general(left_side, right_side, (((0,), (0,)), ((), ())), preferre...  59.6 us
  transfers between devices with their start and end apart: 53, of which 19 were waited for; matrix products, arithmetic and copies ran while one was open for 43% of the time, Pallas kernels for 0%

profile of v1, /device:TPU:0, one launch (start us, length us, event | category | flops | bytes accessed | tf_op | source)
XLA Modules:
  0.0 911.9 jit_solution(15033477507843995306)
XLA Ops:
  23.3 12.9 %collective-permute-done.14 = bf16[192,1152]{1,0:T(8,128)(2,1)S(1)} collective-permute-done((bf16[192,1152]{1,0:T(8,128)(2,1)S(1)}, bf16[192,1152]{1,0:T(8,128)(2,1)S(1)}, u32[]{:S(2)}, u32[]{:S(2)}) %collective-permute-start.14) | collective-permute-done | bytes 442400 | tf_op jit(solution)/shard_map/ppermute | solution.py:135
  55.9 6.9 dynamic_update_slice.24
  77.0 47.3 %collective-permute-done.2 = bf16[192,1152]{1,0:T(8,128)(2,1)S(1)} collective-permute-done((bf16[192,1152]{1,0:T(8,128)(2,1)}, bf16[192,1152]{1,0:T(8,128)(2,1)S(1)}, u32[]{:S(2)}, u32[]{:S(2)}) %collective-permute-start.2) | collective-permute-done | bytes 442400 | tf_op jit(solution)/shard_map/ppermute | solution.py:215
  133.5 15.6 %collective-permute-done.4 = bf16[192,1152]{1,0:T(8,128)(2,1)} collective-permute-done((bf16[192,1152]{1,0:T(8,128)(2,1)S(1)}, bf16[192,1152]{1,0:T(8,128)(2,1)}, u32[]{:S(2)}, u32[]{:S(2)}) %collective-permute-start.4) | collective-permute-done | bytes 442400 | tf_op jit(solution)/shard_map/ppermute | solution.py:215
  161.1 7.5 dynamic_update_slice.26
  184.6 7.6 dynamic_update_slice.29
  193.4 7.5 dynamic_update_slice.30
  270.9 26.7 %collective-permute-done.21 = bf16[2,384,1536]{2,1,0:T(8,128)(2,1)} collective-permute-done((bf16[2,384,1536]{2,1,0:T(8,128)(2,1)S(1)}, bf16[2,384,1536]{2,1,0:T(8,128)(2,1)}, u32[]{:S(2)}, u32[]{:S(2)}) %collective-permute-start.21) | collective-permute-done | bytes 2359328 | tf_op jit(solution)/shard_map/ppermute | solution.py:135
  297.6 8.8 collective-permute-start.24
  321.1 15.6 %collective-permute-done.9 = bf16[2,384,1536]{2,1,0:T(8,128)(2,1)S(1)} collective-permute-done((bf16[2,384,1536]{2,1,0:T(8,128)(2,1)S(1)}, bf16[2,384,1536]{2,1,0:T(8,128)(2,1)S(1)}, u32[]{:S(2)}, u32[]{:S(2)}) %collective-permute-start.9) | collective-permute-done | bytes 2359328 | tf_op jit(solution)/shard_map/ppermute | solution.py:135
  347.4 18.1 %fusion.108 = f32[3072,1152]{1,0:T(8,128)} fusion(bf16[3072,1536]{1,0:T(8,128)(2,1)} %fusion.60, bf16[1536,1152]{1,0:T(8,128)(2,1)} %bitcast.411), kind=kOutput, calls=%fused_computation.273 | convolution fusion | flops 10871635968 | bytes 27131904 | tf_op jit(solution)/shard_map/dot_general | solution.py:54
  365.5 17.9 %fusion.107 = f32[3072,1152]{1,0:T(8,128)} fusion(bf16[3072,1536]{1,0:T(8,128)(2,1)} %fusion.60, bf16[1536,1152]{1,0:T(8,128)(2,1)} %bitcast.414), kind=kOutput, calls=%fused_computation.272 | convolution fusion | flops 10871635968 | bytes 27131904 | tf_op jit(solution)/shard_map/dot_general | solution.py:54
  383.4 6.9 all-gather.14.cloned.1.call-done
  390.3 29.6 %multiply_convert_fusion = (bf16[3072,1152]{1,0:T(8,128)(2,1)}, bf16[3072,1152]{1,0:T(8,128)(2,1)}, bf16[3072,1152]{1,0:T(8,128)(2,1)}) fusion(f32[3072,1152]{1,0:T(8,128)} %fusion.107, f32[3072,1152]{1,0:T(8,128)} %fusion.108, bf16[3072,1536]{1,0:T(8,128)(2,1)} %fusion.56, bf16[1536,1152]{1,0:T(8,128)(2,1)} %bitcast.417), kind=kOutput, calls=%fused_computation.7 | convolution fusion | flops 10924720128 | bytes 62521344 | tf_op jit(solution)/shard_map/dot_general | solution.py:54
  420.0 18.2 %convolution_convert_fusion.1 = bf16[1536,1152]{1,0:T(8,128)(2,1)} fusion(bf16[3072,1536]{1,0:T(8,128)(2,1)} %fusion.56, bf16[3072,1152]{1,0:T(8,128)(2,1)} %get-tuple-element.30), kind=kOutput, calls=%fused_computation.20 | convolution fusion | flops 10873405440 | bytes 20054016 | tf_op jit(solution)/shard_map/dot_general | solution.py:64
  438.2 18.0 %convolution_convert_fusion.2 = bf16[1536,1152]{1,0:T(8,128)(2,1)} fusion(bf16[3072,1536]{1,0:T(8,128)(2,1)} %fusion.60, bf16[3072,1152]{1,0:T(8,128)(2,1)} %get-tuple-element.28), kind=kOutput, calls=%fused_computation.21 | convolution fusion | flops 10873405440 | bytes 20054016 | tf_op jit(solution)/shard_map/dot_general | solution.py:64
  456.2 11.4 %convolution_convert_fusion = bf16[1536,1536]{1,0:T(8,128)(2,1)} fusion(bf16[1536,1152]{1,0:T(8,128)(2,1)} %bitcast.418, bf16[3072,1152]{1,0:T(8,128)(2,1)} %get-tuple-element.30), kind=kOutput, calls=%fused_computation.19 | convolution fusion | flops 5438177280 | bytes 11796480 | tf_op jit(solution)/shard_map/dot_general | solution.py:58
  467.6 11.0 %fusion.14 = f32[1536,1536]{1,0:T(8,128)} fusion(bf16[1536,1152]{1,0:T(8,128)(2,1)S(1)} %bitcast.415, bf16[3072,1152]{1,0:T(8,128)(2,1)} %get-tuple-element.29), kind=kOutput, calls=%fused_computation.37 | convolution fusion | flops 5435817984 | bytes 16515072 | tf_op jit(solution)/shard_map/dot_general | solution.py:58
  478.7 11.7 %add_convert_fusion = bf16[1536,1536]{1,0:T(8,128)(2,1)} fusion(f32[1536,1536]{1,0:T(8,128)} %fusion.14, bf16[1536,1152]{1,0:T(8,128)(2,1)S(1)} %bitcast.413, bf16[3072,1152]{1,0:T(8,128)(2,1)} %get-tuple-element.28), kind=kOutput, calls=%fused_computation.17 | convolution fusion | flops 5440536576 | bytes 21233664 | tf_op jit(solution)/shard_map/dot_general | solution.py:58
  490.8 14.5 %convolution_convert_fusion.3 = bf16[1536,1152]{1,0:T(8,128)(2,1)} fusion(bf16[3072,1536]{1,0:T(8,128)(2,1)S(1)} %bitcast.406, bf16[3072,1152]{1,0:T(8,128)(2,1)S(1)} %bitcast.422), kind=kOutput, calls=%fused_computation.22 | convolution fusion | flops 10873405440 | bytes 20054016 | tf_op jit(solution)/shard_map/dot_general | solution.py:64
  506.1 11.2 %fusion.17 = f32[1536,1536]{1,0:T(8,128)} fusion(bf16[1536,1152]{1,0:T(8,128)(2,1)S(1)} %bitcast.416, bf16[3072,1152]{1,0:T(8,128)(2,1)} %get-tuple-element.29), kind=kOutput, calls=%fused_computation.40 | convolution fusion | flops 5435817984 | bytes 16515072 | tf_op jit(solution)/shard_map/dot_general | solution.py:58
  517.3 9.2 %convert_add_fusion.1 = f32[1536,1536]{1,0:T(8,128)S(1)} fusion(bf16[1536,1536]{1,0:T(8,128)(2,1)} %collective-permute-done.16, bf16[1536,1152]{1,0:T(8,128)(2,1)S(1)} %bitcast.419, bf16[3072,1152]{1,0:T(8,128)(2,1)} %get-tuple-element.30), kind=kOutput, calls=%fused_computation.18 | convolution fusion | flops 5440536576 | bytes 21233664 | tf_op jit(solution)/shard_map/dot_general | solution.py:58
  529.4 12.5 %convert_add_fusion = f32[1536,1536]{1,0:T(8,128)S(1)} fusion(bf16[1536,1536]{1,0:T(8,128)(2,1)} %collective-permute-done.25, f32[1536,1536]{1,0:T(8,128)} %fusion.17, bf16[1536,1152]{1,0:T(8,128)(2,1)} %bitcast.412, bf16[3072,1152]{1,0:T(8,128)(2,1)} %get-tuple-element.28), kind=kOutput, calls=%fused_computation.16 | convolution fusion | flops 5442895872 | bytes 30670848 | tf_op jit(solution)/shard_map/dot_general | solution.py:58
  550.2 29.3 %reduce-scatter.12.cloned.1.call-done = bf16[1,384,1152]{2,1,0:T(8,128)(2,1)} async-done(((bf16[4,384,1152]{2,1,0:T(8,128)(2,1)}), bf16[1,384,1152]{2,1,0:T(8,128)(2,1)}) %reduce-scatter.12.cloned.1.call-update) | async-done | bytes 884752 | tf_op jit(solution)/shard_map/reduce_scatter | solution.py:182
  582.1 66.5 %reduce-scatter.10.cloned.1.call-done = bf16[1,384,1152]{2,1,0:T(8,128)(2,1)} async-done(((bf16[4,384,1152]{2,1,0:T(8,128)(2,1)}), bf16[1,384,1152]{2,1,0:T(8,128)(2,1)}) %reduce-scatter.10.cloned.1.call-update) | async-done | bytes 884752 | tf_op jit(solution)/shard_map/reduce_scatter | solution.py:182
  664.4 22.0 %collective-permute-done.27 = bf16[384,1536]{1,0:T(8,128)(2,1)S(1)} collective-permute-done((bf16[384,1536]{1,0:T(8,128)(2,1)S(1)}, bf16[384,1536]{1,0:T(8,128)(2,1)S(1)}, u32[]{:S(2)}, u32[]{:S(2)}) %collective-permute-start.27) | collective-permute-done | bytes 1179680 | tf_op jit(solution)/shard_map/ppermute | solution.py:135
  690.6 14.7 %collective-permute-start.28 = (bf16[384,1536]{1,0:T(8,128)(2,1)S(1)}, bf16[384,1536]{1,0:T(8,128)(2,1)S(1)}, u32[]{:S(2)}, u32[]{:S(2)}) collective-permute-start(bf16[384,1536]{1,0:T(8,128)(2,1)S(1)} %get-tuple-element.20), channel_id=1, source_target_pairs={{0,1},{1,0},{2,3},{3,2},{4,5},{5,4},{6,7},{7,6},{8,9},{9,8},{10,11... | collective-permute-start | bytes 3538952 | tf_op jit(solution)/shard_map/ppermute | solution.py:135
  712.0 8.8 collective-permute-done.39
  732.9 12.4 %fusion = (f32[6,768]{1,0:T(8,128)S(1)}, f32[768,768,6]{1,0,2:T(8,128)}) fusion(f32[1,6,768,768]{2,3,1,0:T(8,128)} %copy-done, f32[6,768]{1,0:T(8,128)S(1)} %log_add_fusion, bf16[768,6,128]{0,2,1:T(8,128)(2,1)S(1)} %bitcast.387, f32[768,1024]{1,0:T(8,128)} %copy-done.10), kind=kOutput, calls=%fused_computation.3 | convolution fusion | flops 916581888 | bytes 29724672 | tf_op jit(solution)/shard_map/qkgd,skd->kgqs/dot_general | solution.py:293
  747.4 7.8 fusion.9
  783.2 18.5 %collective-permute-start.29 = (bf16[384,1536]{1,0:T(8,128)(2,1)S(1)}, bf16[384,1536]{1,0:T(8,128)(2,1)S(1)}, u32[]{:S(2)}, u32[]{:S(2)}) collective-permute-start(bf16[384,1536]{1,0:T(8,128)(2,1)S(1)} %fusion.53), channel_id=1, source_target_pairs={{0,1},{1,0},{2,3},{3,2},{4,5},{5,4},{6,7},{7,6},{8,9},{9,8},{10,11... | collective-permute-start | bytes 3538952 | tf_op jit(solution)/shard_map/ppermute | solution.py:135
  826.0 67.1 %reduce-scatter.6.cloned.1.call-done = bf16[192,1024]{1,0:T(8,128)(2,1)} async-done(((bf16[1536,1024]{1,0:T(8,128)(2,1)}), bf16[192,1024]{1,0:T(8,128)(2,1)}) %reduce-scatter.6.cloned.1.call-update) | async-done | bytes 393232 | tf_op jit(solution)/shard_map/reduce_scatter | solution.py:192
  (433 shorter events, 302.8 us)
Async XLA Ops:
  7.2 242.8 %all-gather.8.cloned.1.call-start = ((), (), s32[]{:S(2)}) async-start(), calls=%async_computation.5 | async-start | bytes 2654208 | tf_op jit(solution)/shard_map/all_gather | solution.py:225
  7.9 339.5 %all-gather.12.cloned.1.call-start = ((), (), s32[]{:S(2)}) async-start(), calls=%async_computation.12 | async-start | bytes 4423680 | tf_op jit(solution)/shard_map/all_gather | solution.py:177
  37.4 328.1 %all-gather.10.cloned.1.call-start = ((), (), s32[]{:S(2)}) async-start(), calls=%async_computation.11 | async-start | bytes 4423680 | tf_op jit(solution)/shard_map/all_gather | solution.py:177
  38.5 34.0 %collective-permute-start.1 = (bf16[192,1152]{1,0:T(8,128)(2,1)}, bf16[192,1152]{1,0:T(8,128)(2,1)}, u32[]{:S(2)}, u32[]{:S(2)}) collective-permute-start(bf16[192,1152]{1,0:T(8,128)(2,1)} %fusion.73), channel_id=1, source_target_pairs={{0,14},{2,0},{4,2},{6,4},{8,6},{10,8},{12,10},{14,12},{1,15},{3,1}... | collective-permute-start | bytes 1327112 | tf_op jit(solution)/shard_map/ppermute | solution.py:220
  46.6 102.5 %collective-permute-start.13 = (bf16[192,1152]{1,0:T(8,128)(2,1)}, bf16[192,1152]{1,0:T(8,128)(2,1)}, u32[]{:S(2)}, u32[]{:S(2)}) collective-permute-start(bf16[192,1152]{1,0:T(8,128)(2,1)} %bitcast.368), channel_id=1, source_target_pairs={{0,2},{1,3},{2,0},{3,1},{4,6},{5,7},{6,4},{7,5},{8,10},{9,11},{10,... | collective-permute-start | bytes 1327112 | tf_op jit(solution)/shard_map/ppermute | solution.py:135
  49.5 204.5 %collective-permute-start.20 = (bf16[384,1536]{1,0:T(8,128)(2,1)}, bf16[384,1536]{1,0:T(8,128)(2,1)}, u32[]{:S(2)}, u32[]{:S(2)}) collective-permute-start(bf16[384,1536]{1,0:T(8,128)(2,1)} %bitcast.49), channel_id=1, source_target_pairs={{0,2},{1,17},{2,0},{3,19},{4,6},{5,21},{6,4},{7,23},{8,10},{9,25},... | collective-permute-start | bytes 3538952 | tf_op jit(solution)/shard_map/ppermute | solution.py:135
  68.5 55.9 %collective-permute-start.2 = (bf16[192,1152]{1,0:T(8,128)(2,1)}, bf16[192,1152]{1,0:T(8,128)(2,1)S(1)}, u32[]{:S(2)}, u32[]{:S(2)}) collective-permute-start(bf16[192,1152]{1,0:T(8,128)(2,1)} %collective-permute-done), channel_id=1, source_target_pairs={{0,2},{2,4},{4,6},{6,8},{8,10},{10,12},{12,14},{14,0},{1,3},{3,5},... | collective-permute-start | bytes 1327112 | tf_op jit(solution)/shard_map/ppermute | solution.py:215
  72.5 55.4 %collective-permute-start.3 = (bf16[192,1152]{1,0:T(8,128)(2,1)}, bf16[192,1152]{1,0:T(8,128)(2,1)}, u32[]{:S(2)}, u32[]{:S(2)}) collective-permute-start(bf16[192,1152]{1,0:T(8,128)(2,1)} %collective-permute-done.1), channel_id=1, source_target_pairs={{0,14},{2,0},{4,2},{6,4},{8,6},{10,8},{12,10},{14,12},{1,15},{3,1}... | collective-permute-start | bytes 1327112 | tf_op jit(solution)/shard_map/ppermute | solution.py:220
  127.9 64.3 %collective-permute-start.5 = (bf16[192,1152]{1,0:T(8,128)(2,1)}, bf16[192,1152]{1,0:T(8,128)(2,1)}, u32[]{:S(2)}, u32[]{:S(2)}) collective-permute-start(bf16[192,1152]{1,0:T(8,128)(2,1)} %collective-permute-done.3), channel_id=1, source_target_pairs={{0,14},{2,0},{4,2},{6,4},{8,6},{10,8},{12,10},{14,12},{1,15},{3,1}... | collective-permute-start | bytes 1327112 | tf_op jit(solution)/shard_map/ppermute | solution.py:220
  149.1 51.9 %collective-permute-start.6 = (bf16[192,1152]{1,0:T(8,128)(2,1)}, bf16[192,1152]{1,0:T(8,128)(2,1)}, u32[]{:S(2)}, u32[]{:S(2)}) collective-permute-start(bf16[192,1152]{1,0:T(8,128)(2,1)} %collective-permute-done.4), channel_id=1, source_target_pairs={{0,2},{2,4},{4,6},{6,8},{8,10},{10,12},{12,14},{14,0},{1,3},{3,5},... | collective-permute-start | bytes 1327112 | tf_op jit(solution)/shard_map/ppermute | solution.py:215
  151.3 239.1 %all-gather.14.cloned.1.call-start = ((), (), s32[]{:S(2)}) async-start(), calls=%async_computation.13 | async-start | bytes 4423680 | tf_op jit(solution)/shard_map/all_gather | solution.py:177
  256.0 41.7 %collective-permute-start.21 = (bf16[2,384,1536]{2,1,0:T(8,128)(2,1)S(1)}, bf16[2,384,1536]{2,1,0:T(8,128)(2,1)}, u32[]{:S(2)}, u32[]{:S(2)}) collective-permute-start(bf16[2,384,1536]{2,1,0:T(8,128)(2,1)S(1)} %pad_maximum_fusion.2), channel_id=1, source_target_pairs={{0,16},{1,3},{2,18},{3,1},{4,20},{5,7},{6,22},{7,5},{8,24},{9,11},... | collective-permute-start | bytes 7077896 | tf_op jit(solution)/shard_map/ppermute | solution.py:135
  262.0 45.6 %collective-permute-start.8 = (bf16[384,1536]{1,0:T(8,128)(2,1)S(1)}, bf16[384,1536]{1,0:T(8,128)(2,1)S(1)}, u32[]{:S(2)}, u32[]{:S(2)}) collective-permute-start(bf16[384,1536]{1,0:T(8,128)(2,1)S(1)} %get-tuple-element.25), channel_id=1, source_target_pairs={{0,2},{1,17},{2,0},{3,19},{4,6},{5,21},{6,4},{7,23},{8,10},{9,25},... | collective-permute-start | bytes 3538952 | tf_op jit(solution)/shard_map/ppermute | solution.py:135
  264.0 52.6 %collective-permute-start.22 = (bf16[384,1536]{1,0:T(8,128)(2,1)}, bf16[384,1536]{1,0:T(8,128)(2,1)S(1)}, u32[]{:S(2)}, u32[]{:S(2)}) collective-permute-start(bf16[384,1536]{1,0:T(8,128)(2,1)} %bitcast.49), channel_id=1, source_target_pairs={{0,1},{1,0},{2,3},{3,2},{4,5},{5,4},{6,7},{7,6},{8,9},{9,8},{10,11... | collective-permute-start | bytes 3538952 | tf_op jit(solution)/shard_map/ppermute | solution.py:135
  307.4 240.5 %reduce-scatter.14.cloned.1.call-start = ((), (), s32[]{:S(2)}) async-start(), calls=%async_computation.10 | async-start | bytes 4423680 | tf_op jit(solution)/shard_map/reduce_scatter | solution.py:182
  438.1 141.4 %reduce-scatter.12.cloned.1.call-start = ((), (), s32[]{:S(2)}) async-start(), calls=%async_computation.9 | async-start | bytes 4423680 | tf_op jit(solution)/shard_map/reduce_scatter | solution.py:182
  456.2 192.4 %reduce-scatter.10.cloned.1.call-start = ((), (), s32[]{:S(2)}) async-start(), calls=%async_computation.8 | async-start | bytes 4423680 | tf_op jit(solution)/shard_map/reduce_scatter | solution.py:182
  467.6 49.7 %collective-permute-start.16 = (bf16[1536,1536]{1,0:T(8,128)(2,1)}, bf16[1536,1536]{1,0:T(8,128)(2,1)}, u32[]{:S(2)}, u32[]{:S(2)}) collective-permute-start(bf16[1536,1536]{1,0:T(8,128)(2,1)} %convolution_convert_fusion), channel_id=1, source_target_pairs={{0,1},{1,0},{2,3},{3,2},{4,5},{5,4},{6,7},{7,6},{8,9},{9,8},{10,11... | collective-permute-start | bytes 14155784 | tf_op jit(solution)/shard_map/ppermute | solution.py:135
  490.4 39.0 %collective-permute-start.25 = (bf16[1536,1536]{1,0:T(8,128)(2,1)}, bf16[1536,1536]{1,0:T(8,128)(2,1)}, u32[]{:S(2)}, u32[]{:S(2)}) collective-permute-start(bf16[1536,1536]{1,0:T(8,128)(2,1)} %add_convert_fusion), channel_id=1, source_target_pairs={{0,1},{1,0},{2,3},{3,2},{4,5},{5,4},{6,7},{7,6},{8,9},{9,8},{10,11... | collective-permute-start | bytes 14155784 | tf_op jit(solution)/shard_map/ppermute | solution.py:135
  505.4 318.9 %reduce-scatter.8.cloned.1.call-start = ((), (), s32[]{:S(2)}) async-start(), calls=%async_computation.7 | async-start | bytes 2654208 | tf_op jit(solution)/shard_map/reduce_scatter | solution.py:192
  528.2 122.9 %collective-permute-start.17 = (bf16[2,384,1536]{2,1,0:T(8,128)(2,1)}, bf16[2,384,1536]{2,1,0:T(8,128)(2,1)}, u32[]{:S(2)}, u32[]{:S(2)}) collective-permute-start(bf16[2,384,1536]{2,1,0:T(8,128)(2,1)} %bitcast.45), channel_id=1, source_target_pairs={{0,16},{1,3},{2,18},{3,1},{4,20},{5,7},{6,22},{7,5},{8,24},{9,11},... | collective-permute-start | bytes 7077896 | tf_op jit(solution)/shard_map/ppermute | solution.py:135
  543.9 112.1 %collective-permute-start.26 = (bf16[2,384,1536]{2,1,0:T(8,128)(2,1)}, bf16[2,384,1536]{2,1,0:T(8,128)(2,1)}, u32[]{:S(2)}, u32[]{:S(2)}) collective-permute-start(bf16[2,384,1536]{2,1,0:T(8,128)(2,1)} %bitcast.56), channel_id=1, source_target_pairs={{0,16},{1,3},{2,18},{3,1},{4,20},{5,7},{6,22},{7,5},{8,24},{9,11},... | collective-permute-start | bytes 7077896 | tf_op jit(solution)/shard_map/ppermute | solution.py:135
  549.0 111.1 %collective-permute-start.42 = (bf16[192,1152]{1,0:T(8,128)(2,1)S(1)}, bf16[192,1152]{1,0:T(8,128)(2,1)S(1)}, u32[]{:S(2)}, u32[]{:S(2)}) collective-permute-start(bf16[192,1152]{1,0:T(8,128)(2,1)S(1)} %dynamic-slice_bitcast_fusion), channel_id=1, source_target_pairs={{0,2},{1,3},{2,0},{3,1},{4,6},{5,7},{6,4},{7,5},{8,10},{9,11},{10,... | collective-permute-start | bytes 1327112 | tf_op jit(solution)/shard_map/ppermute | solution.py:135
  580.6 81.3 %collective-permute-start.40 = (bf16[192,1152]{1,0:T(8,128)(2,1)S(1)}, bf16[192,1152]{1,0:T(8,128)(2,1)S(1)}, u32[]{:S(2)}, u32[]{:S(2)}) collective-permute-start(bf16[192,1152]{1,0:T(8,128)(2,1)S(1)} %dynamic-slice_bitcast_fusion.1), channel_id=1, source_target_pairs={{0,2},{1,3},{2,0},{3,1},{4,6},{5,7},{6,4},{7,5},{8,10},{9,11},{10,... | collective-permute-start | bytes 1327112 | tf_op jit(solution)/shard_map/ppermute | solution.py:135
  655.3 31.9 %collective-permute-start.18 = (bf16[384,1536]{1,0:T(8,128)(2,1)S(1)}, bf16[384,1536]{1,0:T(8,128)(2,1)S(1)}, u32[]{:S(2)}, u32[]{:S(2)}) collective-permute-start(bf16[384,1536]{1,0:T(8,128)(2,1)S(1)} %fusion.54), channel_id=1, source_target_pairs={{0,2},{1,17},{2,0},{3,19},{4,6},{5,21},{6,4},{7,23},{8,10},{9,25},... | collective-permute-start | bytes 3538952 | tf_op jit(solution)/shard_map/ppermute | solution.py:135
  660.3 44.9 %collective-permute-start.43 = (bf16[2,192,1152]{2,1,0:T(8,128)(2,1)S(1)}, bf16[2,192,1152]{2,1,0:T(8,128)(2,1)}, u32[]{:S(2)}, u32[]{:S(2)}) collective-permute-start(bf16[2,192,1152]{2,1,0:T(8,128)(2,1)S(1)} %pad_maximum_fusion.23), channel_id=1, source_target_pairs={{0,16},{1,17},{2,18},{3,19},{4,20},{5,21},{6,22},{7,23},{8,24},{9,... | collective-permute-start | bytes 2654216 | tf_op jit(solution)/shard_map/ppermute | solution.py:135
  662.1 44.7 %collective-permute-start.41 = (bf16[2,192,1152]{2,1,0:T(8,128)(2,1)S(1)}, bf16[2,192,1152]{2,1,0:T(8,128)(2,1)}, u32[]{:S(2)}, u32[]{:S(2)}) collective-permute-start(bf16[2,192,1152]{2,1,0:T(8,128)(2,1)S(1)} %pad_maximum_fusion.22), channel_id=1, source_target_pairs={{0,16},{1,17},{2,18},{3,19},{4,20},{5,21},{6,22},{7,23},{8,24},{9,... | collective-permute-start | bytes 2654216 | tf_op jit(solution)/shard_map/ppermute | solution.py:135
  662.9 58.0 %collective-permute-start.39 = (bf16[2,192,1152]{2,1,0:T(8,128)(2,1)S(1)}, bf16[2,192,1152]{2,1,0:T(8,128)(2,1)S(1)}, u32[]{:S(2)}, u32[]{:S(2)}) collective-permute-start(bf16[2,192,1152]{2,1,0:T(8,128)(2,1)S(1)} %pad_maximum_fusion.21), channel_id=1, source_target_pairs={{0,16},{1,17},{2,18},{3,19},{4,20},{5,21},{6,22},{7,23},{8,24},{9,... | collective-permute-start | bytes 2654216 | tf_op jit(solution)/shard_map/ppermute | solution.py:135
  690.6 32.6 %collective-permute-start.28 = (bf16[384,1536]{1,0:T(8,128)(2,1)S(1)}, bf16[384,1536]{1,0:T(8,128)(2,1)S(1)}, u32[]{:S(2)}, u32[]{:S(2)}) collective-permute-start(bf16[384,1536]{1,0:T(8,128)(2,1)S(1)} %get-tuple-element.20), channel_id=1, source_target_pairs={{0,1},{1,0},{2,3},{3,2},{4,5},{5,4},{6,7},{7,6},{8,9},{9,8},{10,11... | collective-permute-start | bytes 3538952 | tf_op jit(solution)/shard_map/ppermute | solution.py:135
  705.2 101.3 %collective-permute-start.19 = (bf16[384,1536]{1,0:T(8,128)(2,1)}, bf16[384,1536]{1,0:T(8,128)(2,1)}, u32[]{:S(2)}, u32[]{:S(2)}) collective-permute-start(bf16[384,1536]{1,0:T(8,128)(2,1)} %get-tuple-element.37), channel_id=1, source_target_pairs={{0,1},{1,0},{2,3},{3,2},{4,5},{5,4},{6,7},{7,6},{8,9},{9,8},{10,11... | collective-permute-start | bytes 3538952 | tf_op jit(solution)/shard_map/ppermute | solution.py:135
  728.4 164.7 %reduce-scatter.6.cloned.1.call-start = ((), (), s32[]{:S(2)}) async-start(), calls=%async_computation.6 | async-start | bytes 3538944 | tf_op jit(solution)/shard_map/reduce_scatter | solution.py:192
  824.4 71.8 %collective-permute-start.37 = (bf16[192,768]{1,0:T(8,128)(2,1)}, bf16[192,768]{1,0:T(8,128)(2,1)S(1)}, u32[]{:S(2)}, u32[]{:S(2)}) collective-permute-start(bf16[192,768]{1,0:T(8,128)(2,1)} %reduce-scatter.8.cloned.1.call-done), channel_id=1, source_target_pairs={{0,16},{1,17},{2,18},{3,19},{4,20},{5,21},{6,22},{7,23},{8,24},{9,... | collective-permute-start | bytes 884744 | tf_op jit(solution)/shard_map/ppermute | solution.py:135
  (103 other events, 1462.2 us)
Sparse Core Ops, SparseCore 0:
  10.2 86.3 all-gather.7
  98.2 76.0 all-gather.11
  176.4 76.4 all-gather.9
  307.6 82.7 all-gather.13
  438.3 72.3 reduce-scatter.13
  512.8 66.6 reduce-scatter.11
  581.8 66.6 reduce-scatter.9
  728.5 87.1 reduce-scatter.7
  819.2 73.7 reduce-scatter.5
